TPU v7x, 32 devices: a whole 2x2x4 slice. The times are simulated.
32 devices in a mesh: pairs: 8 (over y, x, core), fit: 4 (over z).
Axes of the slice: x: 2, y: 2, z: 4, core: 2. Of those that a mesh axis runs over, the one named last changes fastest.
Arguments:
- b_first: bfloat16 [64, 160, 3072], P('pairs', None, 'fit'), may hold values from -0.109375 to 0.109375
- b_second: bfloat16 [64, 160, 3072], P('pairs', None, 'fit'), may hold values from -6 to 6
- start_amplitudes: float32 [64, 160, 160], P('pairs'), may hold values from -1.8 to 1.8
- margins: bfloat16 [64, 96, 160, 160], P('pairs', 'fit'), may hold values from -0.5 to 0.5
- fock_terms: float32 [64, 96], P('pairs', 'fit'), may hold values from -0.2 to 0.2
- partners: int32 [64, 96], P('pairs', 'fit'), may hold values from 0 to 63, as said below
- pno_energy: float32 [64, 160], P('pairs'), may hold values from 0.3 to 1.5
- occ_energy: float32 [4000], replicated, may hold values from -1 to -0.2
- pair_list: int32 [64, 2], P('pairs'), may hold values from 0 to 3999
- pno_count: int32 [64], P('pairs'), may hold values from 64 to 160, as said below
Outputs:
- amplitudes: float32 [64, 160, 160], P('pairs')
- residual: float32 [64, 160, 160], P('pairs')
Inputs may be any that keep to these rules, and one draw needn't show every extreme that they name: `pno_count`: each pair's PNO count is one of 64, 128 and 160. `partners`: pairs owner * 8 to owner * 8 + 7 belong to one owner. In the block of one device (its 8 rows and the columns of its index along fit), each owner's pairs appear at most 48 times, and one owner's pairs appear exactly 48 times in every block.
All inputs are finite; a program needn't handle non-finite values.
Results may differ from a plain program's by a relative error of at most 0.0041.
Values may be sent and summed in bfloat16 or wider, within the bound.
A program may use at most 192 MiB of HBM per device.

v0:
```python
import jax
import jax.numpy as jnp
from jax import lax
from jax.sharding import PartitionSpec as P

ITERS = 2


def shards(
    b_first,
    b_second,
    start_amplitudes,
    margins,
    fock_terms,
    partners,
    pno_energy,
    occ_energy,
    pair_list,
    pno_count,
):
    pair_dev = start_amplitudes.shape[0]
    pno_width = pno_energy.shape[1]
    per_pair = partners.shape[1]
    request_count = pair_dev * per_pair
    levels = lax.broadcasted_iota(jnp.int32, (pair_dev, pno_width), 1)
    keep_rows = (levels < pno_count[:, None]).astype(jnp.float32)
    pair_mask = keep_rows[:, :, None] * keep_rows[:, None, :]
    occ_pair = occ_energy[pair_list[:, 0]] + occ_energy[pair_list[:, 1]]
    denominator = pno_energy[:, :, None] + pno_energy[:, None, :] - occ_pair[:, None, None]
    integral_part = jnp.einsum(
        "rap,rbp->rab", b_first, b_second, preferred_element_type=jnp.float32
    )
    flat_partners = partners.reshape(request_count)
    amplitudes = pair_mask * start_amplitudes
    residual = jnp.zeros_like(amplitudes)
    for iteration in range(ITERS):
        rounded = amplitudes.astype(jnp.bfloat16)
        everything = lax.all_gather(rounded, "pairs", axis=0, tiled=True)
        fetched = everything[flat_partners]
        fetched = fetched.reshape(pair_dev, per_pair, pno_width, pno_width)
        left_product = jnp.einsum(
            "rpac,rpcd->rpad", margins, fetched, preferred_element_type=jnp.float32
        ).astype(jnp.bfloat16)
        right_product = jnp.einsum(
            "rpad,rpbd->rpab", left_product, margins, preferred_element_type=jnp.float32
        )
        coupling = jnp.sum(fock_terms[:, :, None, None] * right_product, axis=1)
        partial_sum = integral_part - coupling
        reduced = lax.psum(partial_sum, "fit")
        residual = pair_mask * (reduced + denominator * amplitudes)
        amplitudes = amplitudes - residual / denominator
    return (amplitudes, residual)


def solution(mesh):
    return jax.shard_map(
        shards,
        mesh=mesh,
        in_specs=(
            P("pairs", None, "fit"),
            P("pairs", None, "fit"),
            P("pairs", None, None),
            P("pairs", "fit", None, None),
            P("pairs", "fit"),
            P("pairs", "fit"),
            P("pairs", None),
            P(),
            P("pairs", None),
            P("pairs"),
        ),
        out_specs=(P("pairs", None, None), P("pairs", None, None)),
        check_vma=False,
    )
```

profile of v0, /device:TPU:0, one launch (start us, length us, event | category | flops | bytes accessed | tf_op | source)
XLA Modules:
  0.0 302.1 jit_solution(12965872413875389841)
XLA Ops:
  7.2 0.0 copy-start
  7.2 0.0 all-gather.3.cloned.1.call-start
  7.2 0.9 fusion.15
  8.1 2.4 fusion.14
  10.5 0.0 all-gather.3.cloned.1.call-update
  10.5 0.0 all-reduce.3.cloned.1.call-start
  10.6 0.1 reshape.83
  10.7 0.0 copy-start.8
  10.7 43.7 %all-gather.3.cloned.1.call-done = bf16[64,160,160]{2,1,0:T(8,128)(2,1)} async-done(((bf16[8,160,160]{2,1,0:T(8,128)(2,1)}), bf16[64,160,160]{2,1,0:T(8,128)(2,1)}) %all-gather.3.cloned.1.call-update) | async-done | bytes 3276816 | tf_op jit(solution)/shard_map/all_gather | solution.py:38
  54.4 11.9 %gather_fusion = bf16[192,160,160]{2,1,0:T(8,128)(2,1)} fusion(bf16[64,160,160]{2,1,0:T(8,128)(2,1)} %all-gather.3.cloned.1.call-done, s32[1024]{0:T(1024)S(1)} %pad_clamp_fusion.2), kind=kCustom, calls=%fused_computation | custom fusion | bytes 19661568 | tf_op jit(solution)/shard_map/gather | solution.py:39
  66.3 21.3 %multiply_reduce_fusion.1 = f32[8,160,160]{2,1,0:T(8,128)S(1)} fusion(f32[8,24]{1,0:T(8,128)S(1)} %copy-done.8, bf16[8,24,160,160]{3,2,1,0:T(8,128)(2,1)} %param.13, bf16[8,24,160,160]{3,2,1,0:T(8,128)(2,1)} %bitcast.16), kind=kOutput, calls=%fused_computation.5 | convolution fusion | flops 3160268800 | bytes 20480768 | tf_op jit(solution)/shard_map/rpad,rpbd->rpab/dot_general | solution.py:44
  87.5 0.0 copy-done
  87.5 0.0 copy-start.7
  87.6 0.0 copy-start.2
  87.6 3.7 %fusion.20 = (f32[8,160,160]{2,1,0:T(8,128)}, f32[8,160,160]{2,1,0:T(8,128)}) fusion(f32[8,160,160]{2,1,0:T(8,128)S(1)} %multiply_reduce_fusion.1, bf16[8,160,768]{2,1,0:T(8,128)(2,1)S(1)} %copy-done, bf16[8,160,768]{2,1,0:T(8,128)(2,1)} %param.11), kind=kOutput, calls=%fused_computation.31 | convolution fusion | flops 314777600 | bytes 6389760 | tf_op jit(solution)/shard_map/rap,rbp->rab/dot_general | solution.py:30
  91.3 0.0 all-reduce.3.cloned.1.call-update
  91.3 0.0 all-gather.5.cloned.1.call-start
  91.4 0.0 copy-done.2
  91.4 0.6 gather_fusion.2
  92.1 0.6 gather_fusion.1
  92.7 58.9 %all-reduce.3.cloned.1.call-done = f32[8,160,160]{2,1,0:T(8,128)} async-done(((f32[8,160,160]{2,1,0:T(8,128)}), f32[8,160,160]{2,1,0:T(8,128)}) %all-reduce.3.cloned.1.call-update) | async-done | bytes 819216 | tf_op jit(solution)/shard_map/psum | solution.py:49
  151.6 0.0 copy-done.3
  151.6 2.7 fusion.18
  154.3 0.0 all-gather.5.cloned.1.call-update
  154.3 0.2 all-reduce.5.cloned.1.call-start
  154.5 40.5 %all-gather.5.cloned.1.call-done = bf16[64,160,160]{2,1,0:T(8,128)(2,1)} async-done(((bf16[8,160,160]{2,1,0:T(8,128)(2,1)}), bf16[64,160,160]{2,1,0:T(8,128)(2,1)}) %all-gather.5.cloned.1.call-update) | async-done | bytes 3276816 | tf_op jit(solution)/shard_map/all_gather | solution.py:38
  195.0 11.9 %gather_fusion.3 = bf16[192,160,160]{2,1,0:T(8,128)(2,1)} fusion(bf16[64,160,160]{2,1,0:T(8,128)(2,1)} %all-gather.5.cloned.1.call-done, s32[1024]{0:T(1024)S(1)} %pad_clamp_fusion.2), kind=kCustom, calls=%fused_computation.3 | custom fusion | bytes 19661568 | tf_op jit(solution)/shard_map/gather | solution.py:39
  206.9 22.4 %multiply_reduce_fusion = f32[8,160,160]{2,1,0:T(8,128)} fusion(f32[8,24]{1,0:T(8,128)S(1)} %copy-done.8, bf16[8,24,160,160]{3,2,1,0:T(8,128)(2,1)} %param.13, bf16[8,24,160,160]{3,2,1,0:T(8,128)(2,1)} %bitcast.15), kind=kOutput, calls=%fused_computation.4 | convolution fusion | flops 3160268800 | bytes 20480768 | tf_op jit(solution)/shard_map/rpad,rpbd->rpab/dot_general | solution.py:44
  229.3 2.5 sub.24
  231.8 0.0 all-reduce.5.cloned.1.call-update
  231.9 60.3 %all-reduce.5.cloned.1.call-done = f32[8,160,160]{2,1,0:T(8,128)} async-done(((f32[8,160,160]{2,1,0:T(8,128)}), f32[8,160,160]{2,1,0:T(8,128)}) %all-reduce.5.cloned.1.call-update) | async-done | bytes 819216 | tf_op jit(solution)/shard_map/psum | solution.py:49
  292.1 3.4 %divide_subtract_fusion = (f32[8,160,160]{2,1,0:T(8,128)}, f32[8,160,160]{2,1,0:T(8,128)}) fusion(f32[8,160,160]{2,1,0:T(8,128)S(1)} %get-tuple-element.5, f32[8]{0:T(128)S(1)} %add.55, f32[8,160]{1,0:T(8,128)S(1)} %copy-done.5, f32[8,160,160]{2,1,0:T(8,128)} %all-reduce.5.cloned.1.call-done, f32[8,160]{1,0:T(8,128)S(1)} %fusion.15), kind=kLoop, calls=%fused_computation.17 | loop fusion | flops 1638400 | bytes 3287072 | tf_op jit(solution)/shard_map/sub | solution.py:51
  (16 shorter events, 0.1 us)
Async XLA Ops:
  7.2 80.4 %copy-start = (bf16[8,160,768]{2,1,0:T(8,128)(2,1)S(1)}, bf16[8,160,768]{2,1,0:T(8,128)(2,1)}, u32[]{:S(2)}) copy-start(bf16[8,160,768]{2,1,0:T(8,128)(2,1)} %param.10) | copy-start | bytes 5898244
  7.2 3.4 %copy-start.6 = (s32[8,24]{1,0:T(8,128)S(1)}, s32[8,24]{1,0:T(8,128)}, u32[]{:S(2)}) copy-start(s32[8,24]{1,0:T(8,128)} %param.15) | copy-start | bytes 2308
  7.2 47.2 %all-gather.3.cloned.1.call-start = ((), (), s32[]{:S(2)}) async-start(), calls=%async_computation | async-start | bytes 5898240 | tf_op jit(solution)/shard_map/all_gather | solution.py:38
  10.5 141.1 %all-reduce.3.cloned.1.call-start = ((), (), s32[]{:S(2)}) async-start(), calls=%async_computation.1 | async-start | bytes 2621440 | tf_op jit(solution)/shard_map/psum | solution.py:49
  10.7 55.6 %copy-start.8 = (f32[8,24]{1,0:T(8,128)S(1)}, f32[8,24]{1,0:T(8,128)}, u32[]{:S(2)}) copy-start(f32[8,24]{1,0:T(8,128)} %param.14) | copy-start | bytes 2308
  87.5 3.8 %copy-start.7 = (s32[8,2]{0,1:T(2,128)S(1)}, s32[8,2]{0,1:T(2,128)}, u32[]{:S(2)}) copy-start(s32[8,2]{0,1:T(2,128)} %param.18) | copy-start | bytes 196
  87.6 3.9 %copy-start.2 = (f32[4000]{0:T(1024)S(1)}, f32[4000]{0:T(1024)}, u32[]{:S(2)}) copy-start(f32[4000]{0:T(1024)} %param.17) | copy-start | bytes 48004
  91.3 60.3 %copy-start.3 = (f32[8,160,160]{2,1,0:T(8,128)S(1)}, f32[8,160,160]{2,1,0:T(8,128)}, u32[]{:S(2)}) copy-start(f32[8,160,160]{2,1,0:T(8,128)} %param.12) | copy-start | bytes 2457604
  91.3 60.3 %copy-start.5 = (f32[8,160]{1,0:T(8,128)S(1)}, f32[8,160]{1,0:T(8,128)}, u32[]{:S(2)}) copy-start(f32[8,160]{1,0:T(8,128)} %param.16) | copy-start | bytes 15364
  91.3 103.7 %all-gather.5.cloned.1.call-start = ((), (), s32[]{:S(2)}) async-start(), calls=%async_computation.2 | async-start | bytes 5898240 | tf_op jit(solution)/shard_map/all_gather | solution.py:38
  154.3 137.8 %all-reduce.5.cloned.1.call-start = ((), (), s32[]{:S(2)}) async-start(), calls=%async_computation.3 | async-start | bytes 2621440 | tf_op jit(solution)/shard_map/psum | solution.py:49
  206.9 22.4 %copy-start.4 = (f32[8,160,160]{2,1,0:T(8,128)S(1)}, f32[8,160,160]{2,1,0:T(8,128)}, u32[]{:S(2)}) copy-start(f32[8,160,160]{2,1,0:T(8,128)} %get-tuple-element.9) | copy-start | bytes 2457604
  292.1 3.4 %copy-start.1 = (bf16[8,160,768]{2,1,0:T(8,128)(2,1)S(1)}, bf16[8,160,768]{2,1,0:T(8,128)(2,1)}, u32[]{:S(2)}) copy-start(bf16[8,160,768]{2,1,0:T(8,128)(2,1)} %param.10) | copy-start | bytes 5898244
Sparse Core Ops, SparseCore 0:
  10.6 43.6 all-gather.2
  91.4 60.0 all-reduce.2
  154.4 40.5 all-gather.4
  232.0 60.0 all-reduce.4
where the time goes:
time: 302 us
  waiting for transfers between devices  203 us (67%)
  matrix products  47.4 us (16%)
  local copies, waits for them, and re-layouts  25.2 us (8%)
  between operations  13.9 us (5%)
  other arithmetic  12 us (4%)
    psum x2, waiting for transfers between devices, shards(): reduced = lax.psum(partial_sum, 'fit')  119 us
    all_gather x2, waiting for transfers between devices, shards(): everything = lax.all_gather(rounded, 'pairs', axis=0, tiled=True)  84.2 us
    dot_general x2, matrix products, shards(): jnp.einsum('rpad,rpbd->rpab', left_product, margins, preferred_element_ty...  43.7 us
    gather x2, local copies, waits for them, and re-layouts, shards(): fetched = everything[flat_partners]  23.7 us
  transfers between devices with their start and end apart: 4, of which 4 were waited for; matrix products, arithmetic and copies ran while one was open for 0% of the time, Pallas kernels for 0%

commit v1 on v0

--- a/solution.py
+++ b/solution.py
@@ -46,7 +46,9 @@
         )
         coupling = jnp.sum(fock_terms[:, :, None, None] * right_product, axis=1)
         partial_sum = integral_part - coupling
-        reduced = lax.psum(partial_sum, "fit")
+        reduced = partial_sum
+        for hop in (1, 2):
+            reduced = reduced + lax.ppermute(reduced, "fit", [(dev, dev ^ hop) for dev in range(4)])
         residual = pair_mask * (reduced + denominator * amplitudes)
         amplitudes = amplitudes - residual / denominator
     return (amplitudes, residual)

time: 302 us -> 361 us (1.20)
  waiting for transfers between devices: 203 us -> 256 us
  starting transfers between devices: 0.34 us -> 8.11 us
    ppermute x0 -> x4, waiting for transfers between devices: none -> 171 us  [shards(): lax.ppermute(reduced, 'fit', [(dev, dev ^ hop) for dev in range(4)])]
    psum x2 -> x0, waiting for transfers between devices: 119 us -> none  [shards(): reduced = lax.psum(partial_sum, 'fit')]
    ppermute x0 -> x4, starting transfers between devices: none -> 8.03 us  [shards(): lax.ppermute(reduced, 'fit', [(dev, dev ^ hop) for dev in range(4)])]
  transfers between devices with their start and end apart: 4 -> 6, of which waited for: 4 -> 6; matrix products, arithmetic and copies ran while one was open for 0% -> 0% of each run, Pallas kernels for 0% -> 0%
where the time goes in v1:
time: 361 us
  waiting for transfers between devices  256 us (71%)
  matrix products  46.9 us (13%)
  local copies, waits for them, and re-layouts  25.2 us (7%)
  between operations  14.1 us (4%)
  other arithmetic  10.9 us (3%)
  starting transfers between devices  8.11 us (2%)
    ppermute x4, waiting for transfers between devices, shards(): lax.ppermute(reduced, 'fit', [(dev, dev ^ hop) for dev in range(4)])  171 us
    all_gather x2, waiting for transfers between devices, shards(): everything = lax.all_gather(rounded, 'pairs', axis=0, tiled=True)  84.9 us
    dot_general x2, matrix products, shards(): jnp.einsum('rpad,rpbd->rpab', left_product, margins, preferred_element_ty...  43.6 us
    gather x2, local copies, waits for them, and re-layouts, shards(): fetched = everything[flat_partners]  23.8 us
    ppermute x4, starting transfers between devices, shards(): lax.ppermute(reduced, 'fit', [(dev, dev ^ hop) for dev in range(4)])  8.03 us
  transfers between devices with their start and end apart: 6, of which 6 were waited for; matrix products, arithmetic and copies ran while one was open for 0% of the time, Pallas kernels for 0%

profile of v1, /device:TPU:0, one launch (start us, length us, event | category | flops | bytes accessed | tf_op | source)
XLA Modules:
  0.0 360.9 jit_solution(15766291592038929095)
XLA Ops:
  7.2 0.0 copy-start
  7.2 0.0 all-gather.3.cloned.1.call-start
  7.2 0.9 fusion.15
  8.1 2.4 fusion.14
  10.5 0.0 all-gather.3.cloned.1.call-update
  10.5 0.0 all-gather.5.cloned.1.call-start
  10.6 0.1 reshape.83
  10.7 0.0 copy-start.8
  10.7 43.7 %all-gather.3.cloned.1.call-done = bf16[64,160,160]{2,1,0:T(8,128)(2,1)} async-done(((bf16[8,160,160]{2,1,0:T(8,128)(2,1)}), bf16[64,160,160]{2,1,0:T(8,128)(2,1)}) %all-gather.3.cloned.1.call-update) | async-done | bytes 3276816 | tf_op jit(solution)/shard_map/all_gather | solution.py:38
  54.4 11.9 %gather_fusion = bf16[192,160,160]{2,1,0:T(8,128)(2,1)} fusion(bf16[64,160,160]{2,1,0:T(8,128)(2,1)} %all-gather.3.cloned.1.call-done, s32[1024]{0:T(1024)S(1)} %pad_clamp_fusion.2), kind=kCustom, calls=%fused_computation | custom fusion | bytes 19661568 | tf_op jit(solution)/shard_map/gather | solution.py:39
  66.3 21.3 %multiply_reduce_fusion.1 = f32[8,160,160]{2,1,0:T(8,128)S(1)} fusion(f32[8,24]{1,0:T(8,128)S(1)} %copy-done.8, bf16[8,24,160,160]{3,2,1,0:T(8,128)(2,1)} %param.13, bf16[8,24,160,160]{3,2,1,0:T(8,128)(2,1)} %bitcast.16), kind=kOutput, calls=%fused_computation.5 | convolution fusion | flops 3160268800 | bytes 20480768 | tf_op jit(solution)/shard_map/rpad,rpbd->rpab/dot_general | solution.py:44
  87.6 3.3 fusion.20
  90.9 1.5 collective-permute-start
  92.4 29.4 %collective-permute-done = f32[8,160,160]{2,1,0:T(8,128)S(1)} collective-permute-done((f32[8,160,160]{2,1,0:T(8,128)S(1)}, f32[8,160,160]{2,1,0:T(8,128)S(1)}, u32[]{:S(2)}, u32[]{:S(2)}) %collective-permute-start) | collective-permute-done | bytes 819232 | tf_op jit(solution)/shard_map/ppermute | solution.py:51
  121.8 0.2 add.58
  122.0 0.0 copy-start.4
  122.0 2.5 collective-permute-start.1
  124.6 0.6 gather_fusion.2
  125.2 0.6 gather_fusion.1
  125.9 55.4 %collective-permute-done.1 = f32[8,160,160]{2,1,0:T(8,128)} collective-permute-done((f32[8,160,160]{2,1,0:T(8,128)S(1)}, f32[8,160,160]{2,1,0:T(8,128)}, u32[]{:S(2)}, u32[]{:S(2)}) %collective-permute-start.1) | collective-permute-done | bytes 819232 | tf_op jit(solution)/shard_map/ppermute | solution.py:51
  181.2 3.2 fusion.18
  184.4 0.0 all-gather.5.cloned.1.call-update
  184.4 41.2 %all-gather.5.cloned.1.call-done = bf16[64,160,160]{2,1,0:T(8,128)(2,1)} async-done(((bf16[8,160,160]{2,1,0:T(8,128)(2,1)}), bf16[64,160,160]{2,1,0:T(8,128)(2,1)}) %all-gather.5.cloned.1.call-update) | async-done | bytes 3276816 | tf_op jit(solution)/shard_map/all_gather | solution.py:38
  225.6 11.9 %gather_fusion.3 = bf16[192,160,160]{2,1,0:T(8,128)(2,1)} fusion(bf16[64,160,160]{2,1,0:T(8,128)(2,1)} %all-gather.5.cloned.1.call-done, s32[1024]{0:T(1024)S(1)} %pad_clamp_fusion.2), kind=kCustom, calls=%fused_computation.3 | custom fusion | bytes 19661568 | tf_op jit(solution)/shard_map/gather | solution.py:39
  237.5 22.3 %multiply_reduce_fusion = f32[8,160,160]{2,1,0:T(8,128)} fusion(f32[8,24]{1,0:T(8,128)S(1)} %copy-done.8, bf16[8,24,160,160]{3,2,1,0:T(8,128)(2,1)} %param.13, bf16[8,24,160,160]{3,2,1,0:T(8,128)(2,1)} %bitcast.15), kind=kOutput, calls=%fused_computation.4 | convolution fusion | flops 3160268800 | bytes 20480768 | tf_op jit(solution)/shard_map/rpad,rpbd->rpab/dot_general | solution.py:44
  259.8 1.9 sub.24
  261.7 1.6 collective-permute-start.2
  263.3 29.4 %collective-permute-done.2 = f32[8,160,160]{2,1,0:T(8,128)S(1)} collective-permute-done((f32[8,160,160]{2,1,0:T(8,128)S(1)}, f32[8,160,160]{2,1,0:T(8,128)S(1)}, u32[]{:S(2)}, u32[]{:S(2)}) %collective-permute-start.2) | collective-permute-done | bytes 819232 | tf_op jit(solution)/shard_map/ppermute | solution.py:51
  292.7 0.2 add.67
  292.9 2.5 collective-permute-start.3
  295.4 56.6 %collective-permute-done.3 = f32[8,160,160]{2,1,0:T(8,128)S(1)} collective-permute-done((f32[8,160,160]{2,1,0:T(8,128)S(1)}, f32[8,160,160]{2,1,0:T(8,128)S(1)}, u32[]{:S(2)}, u32[]{:S(2)}) %collective-permute-start.3) | collective-permute-done | bytes 819232 | tf_op jit(solution)/shard_map/ppermute | solution.py:51
  352.0 2.1 divide_subtract_fusion
  (20 shorter events, 0.1 us)
Async XLA Ops:
  7.2 80.4 %copy-start = (bf16[8,160,768]{2,1,0:T(8,128)(2,1)S(1)}, bf16[8,160,768]{2,1,0:T(8,128)(2,1)}, u32[]{:S(2)}) copy-start(bf16[8,160,768]{2,1,0:T(8,128)(2,1)} %param.10) | copy-start | bytes 5898244
  7.2 47.2 %all-gather.3.cloned.1.call-start = ((), (), s32[]{:S(2)}) async-start(), calls=%async_computation | async-start | bytes 5898240 | tf_op jit(solution)/shard_map/all_gather | solution.py:38
  8.1 2.5 copy-start.6
  10.5 215.1 %all-gather.5.cloned.1.call-start = ((), (), s32[]{:S(2)}) async-start(), calls=%async_computation.1 | async-start | bytes 5898240 | tf_op jit(solution)/shard_map/all_gather | solution.py:38
  10.7 55.6 %copy-start.8 = (f32[8,24]{1,0:T(8,128)S(1)}, f32[8,24]{1,0:T(8,128)}, u32[]{:S(2)}) copy-start(f32[8,24]{1,0:T(8,128)} %param.14) | copy-start | bytes 2308
  90.9 33.7 %copy-start.7 = (s32[8,2]{0,1:T(2,128)S(1)}, s32[8,2]{0,1:T(2,128)}, u32[]{:S(2)}) copy-start(s32[8,2]{0,1:T(2,128)} %param.18) | copy-start | bytes 196
  90.9 33.7 %copy-start.2 = (f32[4000]{0:T(1024)S(1)}, f32[4000]{0:T(1024)}, u32[]{:S(2)}) copy-start(f32[4000]{0:T(1024)} %param.17) | copy-start | bytes 48004
  90.9 90.4 %copy-start.5 = (f32[8,160]{1,0:T(8,128)S(1)}, f32[8,160]{1,0:T(8,128)}, u32[]{:S(2)}) copy-start(f32[8,160]{1,0:T(8,128)} %param.16) | copy-start | bytes 15364
  90.9 30.9 %collective-permute-start = (f32[8,160,160]{2,1,0:T(8,128)S(1)}, f32[8,160,160]{2,1,0:T(8,128)S(1)}, u32[]{:S(2)}, u32[]{:S(2)}) collective-permute-start(f32[8,160,160]{2,1,0:T(8,128)S(1)} %get-tuple-element.8), channel_id=1, source_target_pairs={{0,1},{1,0},{2,3},{3,2},{4,5},{5,4},{6,7},{7,6},{8,9},{9,8},{10,11... | collective-permute-start | bytes 2457608 | tf_op jit(solution)/shard_map/ppermute | solution.py:51
  121.8 59.5 %copy-start.3 = (f32[8,160,160]{2,1,0:T(8,128)S(1)}, f32[8,160,160]{2,1,0:T(8,128)}, u32[]{:S(2)}) copy-start(f32[8,160,160]{2,1,0:T(8,128)} %param.12) | copy-start | bytes 2457604
  122.0 3.8 %copy-start.4 = (f32[8,160,160]{2,1,0:T(8,128)}, f32[8,160,160]{2,1,0:T(8,128)S(1)}, u32[]{:S(2)}) copy-start(f32[8,160,160]{2,1,0:T(8,128)S(1)} %add.58) | copy-start | bytes 2457604
  122.0 59.2 %collective-permute-start.1 = (f32[8,160,160]{2,1,0:T(8,128)S(1)}, f32[8,160,160]{2,1,0:T(8,128)}, u32[]{:S(2)}, u32[]{:S(2)}) collective-permute-start(f32[8,160,160]{2,1,0:T(8,128)S(1)} %add.58), channel_id=1, source_target_pairs={{0,2},{1,3},{2,0},{3,1},{4,6},{5,7},{6,4},{7,5},{8,10},{9,11},{10,... | collective-permute-start | bytes 2457608 | tf_op jit(solution)/shard_map/ppermute | solution.py:51
  261.7 31.0 %collective-permute-start.2 = (f32[8,160,160]{2,1,0:T(8,128)S(1)}, f32[8,160,160]{2,1,0:T(8,128)S(1)}, u32[]{:S(2)}, u32[]{:S(2)}) collective-permute-start(f32[8,160,160]{2,1,0:T(8,128)S(1)} %sub.24), channel_id=1, source_target_pairs={{0,1},{1,0},{2,3},{3,2},{4,5},{5,4},{6,7},{7,6},{8,9},{9,8},{10,11... | collective-permute-start | bytes 2457608 | tf_op jit(solution)/shard_map/ppermute | solution.py:51
  292.9 59.1 %collective-permute-start.3 = (f32[8,160,160]{2,1,0:T(8,128)S(1)}, f32[8,160,160]{2,1,0:T(8,128)S(1)}, u32[]{:S(2)}, u32[]{:S(2)}) collective-permute-start(f32[8,160,160]{2,1,0:T(8,128)S(1)} %add.67), channel_id=1, source_target_pairs={{0,2},{1,3},{2,0},{3,1},{4,6},{5,7},{6,4},{7,5},{8,10},{9,11},{10,... | collective-permute-start | bytes 2457608 | tf_op jit(solution)/shard_map/ppermute | solution.py:51
  352.0 2.1 copy-start.1
Sparse Core Ops, SparseCore 0:
  10.6 43.6 all-gather.2
  184.6 40.9 all-gather.4
